TPU v7x, 32 devices: a whole 2x2x4 slice. The times are simulated.
32 devices in a mesh: gx: 4 (over y, x), gy: 8 (over z, core).
Axes of the slice: x: 2, y: 2, z: 4, core: 2. Of those that a mesh axis runs over, the one named last changes fastest.
Arguments:
- old_state: float32 [8, 8, 128, 1024], P(None, None, 'gx', 'gy'), may hold values from -6 to 6
- section_prims: float32 [8, 8, 128, 1024], P(None, None, 'gx', 'gy'), may hold values from -3 to 3, as said below
- shear_whole: int32 [1], replicated, may hold values from 0 to 1023
- shear_frac: float32 [1], replicated, may hold values from 0 to 1
Outputs:
- new_state: float32 [8, 8, 128, 1024], P(None, None, 'gx', 'gy')
Inputs may be any that keep to these rules, and one draw needn't show every extreme that they name: section_prims holds density in [0.5, 2] in field 0 and pressure in [0.3, 3] in field 4; the other fields lie in the stated range.
All inputs are finite; a program needn't handle non-finite values.
Results may differ from a plain program's by a relative error of at most 0.0003.
Values sent between devices are 32-bit elements; how exact they have to be, the bound alone decides.
No kernel may reach another device: no remote copies, remote signals or barrier semaphores. Data moves between devices by JAX's collectives and lax.ppermute only.
A program may use at most 128 MiB of HBM per device.

v0:
```python
import jax
import jax.numpy as jnp
from jax import lax
from jax.sharding import PartitionSpec as P

gamma_gas = 5.0 / 3.0
omega_rate = 1.0
shear_rate = 1.5
time_step = 0.1


def with_halo(shard, sides, width):
    for axis, dim in sides:
        size, length = (lax.axis_size(axis), shard.shape[dim])
        up = [(i, (i + 1) % size) for i in range(size)]
        down = [(j, i) for i, j in up]
        last = lax.slice_in_dim(shard, length - width, length, axis=dim)
        first = lax.slice_in_dim(shard, 0, width, axis=dim)
        before = lax.ppermute(last, axis, up)
        after = lax.ppermute(first, axis, down)
        shard = jnp.concatenate([before, shard, after], axis=dim)
    return shard


def conserved(prims):
    rho = prims[0]
    kinetic = 0.5 * rho * (prims[1] * prims[1] + prims[2] * prims[2] + prims[3] * prims[3])
    magnetic = 0.5 * (prims[5] * prims[5] + prims[6] * prims[6] + prims[7] * prims[7])
    energy = prims[4] / (gamma_gas - 1.0) + kinetic + magnetic
    return jnp.stack(
        [rho, rho * prims[1], rho * prims[2], rho * prims[3], energy, prims[5], prims[6], prims[7]]
    )


def fluxes(prims, cons, direction):
    rho = prims[0]
    normal_vel = prims[1 + direction]
    normal_mag = prims[5 + direction]
    ptotal = prims[4] + 0.5 * (prims[5] * prims[5] + prims[6] * prims[6] + prims[7] * prims[7])
    vdotb = prims[1] * prims[5] + prims[2] * prims[6] + prims[3] * prims[7]
    parts = [rho * normal_vel]
    for comp in range(3):
        parts.append(rho * prims[1 + comp] * normal_vel - prims[5 + comp] * normal_mag)
    parts[1 + direction] = parts[1 + direction] + ptotal
    parts.append((cons[4] + ptotal) * normal_vel - normal_mag * vdotb)
    for comp in range(3):
        parts.append(prims[5 + comp] * normal_vel - prims[1 + comp] * normal_mag)
    return jnp.stack(parts)


def fast_speed(prims, direction):
    rho = prims[0]
    sound = gamma_gas * prims[4] / rho
    squares = [prims[5] * prims[5], prims[6] * prims[6], prims[7] * prims[7]]
    alfven = (squares[0] + squares[1] + squares[2]) / rho
    others = [squares[c] for c in range(3) if c != direction]
    transverse = (others[0] + others[1]) / rho
    disc = jnp.square(sound - alfven) + 4.0 * sound * transverse
    return jnp.sqrt(0.5 * (sound + alfven + jnp.sqrt(disc)))


def minmod(first, second):
    return 0.5 * (jnp.sign(first) + jnp.sign(second)) * jnp.minimum(jnp.abs(first), jnp.abs(second))


def rusanov(left, right, direction):
    cons_left = conserved(left)
    cons_right = conserved(right)
    flux_left = fluxes(left, cons_left, direction)
    flux_right = fluxes(right, cons_right, direction)
    speed_left = jnp.abs(left[1 + direction]) + fast_speed(left, direction)
    speed_right = jnp.abs(right[1 + direction]) + fast_speed(right, direction)
    speed = jnp.maximum(speed_left, speed_right)
    return 0.5 * (flux_left + flux_right) - 0.5 * speed * (cons_right - cons_left)


def sweep(padded, axis, direction):
    length = padded.shape[axis]
    cells = length - 4

    def take(arr, start, stop):
        return lax.slice_in_dim(arr, start, stop, axis=axis)

    diff = take(padded, 1, length) - take(padded, 0, length - 1)
    slope = minmod(take(diff, 0, length - 2), take(diff, 1, length - 1))
    left = take(padded, 1, length - 2) + 0.5 * take(slope, 0, length - 3)
    right = take(padded, 2, length - 1) - 0.5 * take(slope, 1, length - 2)
    face = rusanov(left, right, direction)
    return take(face, 1, cells + 1) - take(face, 0, cells)


def sources(core):
    rho = core[0]
    zeros = jnp.zeros_like(rho)
    return jnp.stack(
        [
            zeros,
            2.0 * omega_rate * rho * core[2],
            -(2.0 - shear_rate) * omega_rate * rho * core[1],
            zeros,
            shear_rate * omega_rate * (rho * core[1] * core[2] - core[5] * core[6]),
            zeros,
            -shear_rate * omega_rate * core[5],
            zeros,
        ]
    )


def section_update(radial_rows, azimuthal_rows, old):
    core = azimuthal_rows[:, :, :, 2:-2]
    radial = sweep(radial_rows, 2, 0)
    azimuthal = sweep(azimuthal_rows, 3, 1)
    zpadded = jnp.concatenate([core[:, -2:], core, core[:, :2]], axis=1)
    vertical = sweep(zpadded, 1, 2)
    rates = -(radial + azimuthal + vertical) + sources(core)
    return 0.5 * old + 0.5 * (conserved(core) + time_step * rates)


def on_device(old_state, section_prims, shear_whole, shear_frac):
    padded = with_halo(section_prims, (("gx", 2), ("gy", 3)), 2)
    cells = section_prims.shape[3]
    loop_size = lax.axis_size("gy")
    total = cells * loop_size
    shift_cells = shear_whole[0]
    frac = shear_frac[0]
    back_cells = (total - 1 - shift_cells) % total
    inner_src = padded[:, :, 0:2, 2:-2]
    outer_src = padded[:, :, -2:, 2:-2]
    inner_cycle, outer_cycle = (
        lax.all_gather(inner_src, "gy", axis=3, tiled=True),
        lax.all_gather(outer_src, "gy", axis=3, tiled=True),
    )
    position = lax.axis_index("gy") * cells
    inner_ext = jnp.concatenate([inner_cycle, inner_cycle[..., : cells + 1]], axis=3)
    outer_ext = jnp.concatenate([outer_cycle, outer_cycle[..., : cells + 1]], axis=3)
    inner_win = lax.dynamic_slice_in_dim(inner_ext, (position + shift_cells) % total, cells + 1, 3)
    outer_win = lax.dynamic_slice_in_dim(outer_ext, (position + back_cells) % total, cells + 1, 3)
    inner_ghost = (1.0 - frac) * inner_win[..., :cells] + frac * inner_win[..., 1:]
    outer_ghost = (1.0 - frac) * outer_win[..., 1:] + frac * outer_win[..., :cells]
    radial_index = lax.axis_index("gx")
    left_rows = jnp.where(radial_index == 0, inner_ghost, inner_src)
    right_rows = jnp.where(radial_index == lax.axis_size("gx") - 1, outer_ghost, outer_src)
    azimuthal_rows = padded[:, :, 2:-2, :]
    radial_rows = jnp.concatenate([left_rows, azimuthal_rows[:, :, :, 2:-2], right_rows], axis=2)
    return section_update(radial_rows, azimuthal_rows, old_state)


def solution(mesh):
    in_specs = (P(None, None, "gx", "gy"), P(None, None, "gx", "gy"), P(), P())
    out_specs = P(None, None, "gx", "gy")
    return jax.shard_map(
        on_device, mesh=mesh, in_specs=in_specs, out_specs=out_specs, check_vma=False
    )
```

profile of v0, /device:TPU:0, one launch (start us, length us, event | category | flops | bytes accessed | tf_op | source)
XLA Modules:
  0.0 111.1 jit_solution(10720879476394507808)
XLA Ops:
  0.0 1.9 %copy.188 = f32[8,8,32,128]{3,1,2,0:T(8,128)S(1)} copy(f32[8,8,32,128]{3,2,1,0:T(8,128)} %param.5) | data formatting | bytes 2097152 | tf_op args[1]
  1.9 1.0 copy-done.4
  3.6 3.9 %collective-permute-start.1 = (f32[8,8,2,128]{3,1,2,0:T(8,128)}, f32[8,8,2,128]{3,1,2,0:T(8,128)S(1)}, u32[]{:S(2)}, u32[]{:S(2)}) collective-permute-start(f32[8,8,2,128]{3,1,2,0:T(8,128)} %get-tuple-element.78), channel_id=1, source_target_pairs={{8,0},{16,8},{24,16},{0,24},{9,1},{17,9},{25,17},{1,25},{10,2},{18... | collective-permute-start | bytes 196616 | tf_op jit(solution)/shard_map/ppermute | solution.py:20
  8.4 1.7 %pad_maximum_fusion.5 = (f32[8,9,32,128]{3,2,1,0:T(8,128)}, f32[8,9,32,128]{3,2,1,0:T(8,128)}) fusion(f32[8,8,32,128]{3,2,1,0:T(8,128)S(1)} %copy-done.1, f32[8,2,32,128]{3,2,1,0:T(8,128)S(1)} %get-tuple-element.82, f32[8,2,32,128]{3,2,1,0:T(8,128)S(1)} %get-tuple-element.83), kind=kLoop, calls=%fused_computation.19 | loop fusion | flops 589824 | bytes 3932160 | tf_op jit(solution)/shard_map/concatenate | solution.py:113
  12.4 2.1 %copy_subtract_fusion = f32[8,11,32,128]{3,1,2,0:T(8,128)S(1)} fusion(f32[8,11,32,128]{3,2,1,0:T(8,128)S(1)} %get-tuple-element.51, f32[8,11,32,128]{3,2,1,0:T(8,128)S(1)} %get-tuple-element.50), kind=kLoop, calls=%fused_computation.12 | loop fusion | flops 360448 | bytes 4325376 | tf_op jit(solution)/shard_map/sub | solution.py:84
  14.5 1.5 %minimum_multiply_fusion = f32[8,10,32,128]{3,1,2,0:T(8,128)S(1)} fusion(f32[8,11,32,128]{3,1,2,0:T(8,128)S(1)} %copy_subtract_fusion), kind=kLoop, calls=%fused_computation.14 | loop fusion | flops 2621440 | bytes 3932160 | tf_op jit(solution)/shard_map/mul | solution.py:63
  16.1 2.2 %fusion.1 = (f32[8,9,32,128]{3,1,2,0:T(8,128)S(1)}, f32[8,9,32,128]{3,1,2,0:T(8,128)S(1)}) fusion(f32[8,10,32,128]{3,1,2,0:T(8,128)S(1)} %minimum_multiply_fusion, f32[8,9,32,128]{3,2,1,0:T(8,128)S(1)} %copy-done.8, f32[8,9,32,128]{3,2,1,0:T(8,128)S(1)} %copy-done.9), kind=kLoop, calls=%fused_computation.4 | loop fusion | flops 1179648 | bytes 7077888 | tf_op jit(solution)/shard_map/add | solution.py:86
  18.5 1.3 %multiply_bitcast_fusion = (f32[9,32,128]{2,0,1:T(8,128)}, f32[1,9,32,128]{3,1,2,0:T(8,128)S(1)}, f32[1,9,32,128]{3,1,2,0:T(8,128)S(1)}, f32[8,9,32,128]{3,1,2,0:T(8,128)S(1)}) fusion(f32[8,9,32,128]{3,1,2,0:T(8,128)S(1)} %get-tuple-element.49, f32[8,9,32,128]{3,1,2,0:T(8,128)S(1)} %get-tuple-element.48, ...), kind=kLoop, calls=%fused_computation.52 | loop fusion | flops 1622016 | bytes 4341760 | tf_op jit(solution)/shard_map/mul | solution.py:74
  20.5 0.7 subtract_dynamic-update-slice_fusion
  21.3 0.8 constant_dynamic-update-slice_fusion.51
  22.0 0.7 constant_dynamic-update-slice_fusion.50
  22.8 0.7 constant_dynamic-update-slice_fusion.49
  23.6 0.9 subtract_dynamic-update-slice_fusion.9
  24.6 0.8 subtract_dynamic-update-slice_fusion.6
  25.4 0.8 constant_dynamic-update-slice_fusion.56
  26.2 0.7 constant_dynamic-update-slice_fusion.55
  26.9 0.8 constant_dynamic-update-slice_fusion.54
  27.7 0.7 constant_dynamic-update-slice_fusion.64
  28.4 0.8 constant_dynamic-update-slice_fusion.63
  29.8 0.8 constant_dynamic-update-slice_fusion.61
  31.2 0.8 constant_dynamic-update-slice_fusion.59
  32.0 0.8 slice_dynamic-update-slice_fusion.6
  32.9 0.7 constant_dynamic-update-slice_fusion.48
  33.6 2.1 %constant_dynamic-update-slice_fusion.53 = f32[8,9,32,128]{3,1,2,0:T(8,128)} fusion(f32[8,9,32,128]{3,1,2,0:T(8,128)} %constant_dynamic-update-slice_fusion.54, f32[1,9,32,128]{3,1,2,0:T(8,128)} %get-tuple-element.25), kind=kLoop, calls=%fused_computation.157 | loop fusion | bytes 524288
  35.7 2.5 %slice_dynamic-update-slice_fusion = (f32[8,9,32,128]{3,1,2,0:T(8,128)}, f32[8,9,32,128]{3,1,2,0:T(8,128)}) fusion(f32[8,9,32,128]{3,1,2,0:T(8,128)} %constant_dynamic-update-slice_fusion.53, f32[8,9,32,128]{3,1,2,0:T(8,128)} %copy-done, f32[8,9,32,128]{3,1,2,0:T(8,128)} %constant_dynamic-update-slice_fusion.48, f32[8,9,32,128]{3,1,2,0:T(8,128)S(1)} %get-tuple-element.49), kind=kLoop, calls=%fused_computation.41 | loop fusion | bytes 2801664 | tf_op jit(solution)/shard_map/stack | solution.py:30
  38.2 4.1 %multiply_subtract_fusion = f32[8,9,32,128]{3,1,2,0:T(8,128)} fusion(f32[8,9,32,128]{3,1,2,0:T(8,128)} %get-tuple-element.89, f32[8,9,32,128]{3,1,2,0:T(8,128)} %get-tuple-element.88, f32[8,9,32,128]{3,1,2,0:T(8,128)S(1)} %copy-done.13, f32[8,9,32,128]{3,1,2,0:T(8,128)S(1)} %copy-done.11, f32[9,32,128]{2,0,1:T(8,128)} %get-tuple-element.19), kind=kLoop, calls=%fused_computation.13 | loop fusion | flops 1474560 | bytes 6045696 | tf_op jit(solution)/shard_map/sub | solution.py:74
  43.0 15.0 %all_gather.7 = f32[8,8,2,1024]{3,1,2,0:T(8,128)S(1)} all-gather(f32[8,8,2,128]{3,1,2,0:T(8,128)S(1)} %collective-permute-done.1), channel_id=1, replica_groups=mesh['gx'=4,'gy'=8] {'gy'}, dimensions={3}, use_global_device_ids=true | all-gather | bytes 589824 | tf_op jit(solution)/shard_map/all_gather | solution.py:131
  58.1 15.1 %all_gather.6 = f32[8,8,2,1024]{3,1,2,0:T(8,128)S(1)} all-gather(f32[8,8,2,128]{3,1,2,0:T(8,128)S(1)} %collective-permute-done), channel_id=1, replica_groups=mesh['gx'=4,'gy'=8] {'gy'}, dimensions={3}, use_global_device_ids=true | all-gather | bytes 589824 | tf_op jit(solution)/shard_map/all_gather | solution.py:130
  75.2 0.9 multiply_bitcast_fusion.2
  76.2 0.7 constant_dynamic-update-slice_fusion.16
  77.1 1.0 constant_dynamic-update-slice_fusion.8
  78.1 1.0 copy-done.16
  79.1 1.4 %fusion.21 = (f32[8,8,36,2]{3,1,2,0:T(8,128)}, f32[8,8,36,2]{3,1,2,0:T(8,128)S(1)}) fusion(f32[8,8,36,128]{3,1,2,0:T(8,128)S(1)} %get-tuple-element.87), kind=kLoop, calls=%fused_computation.205 | loop fusion | bytes 73728 | tf_op jit(solution)/shard_map/slice | solution.py:17
  80.5 1.8 %copy.194 = f32[8,8,36,2]{2,1,3,0:T(8,128)S(1)} copy(f32[8,8,36,2]{3,1,2,0:T(8,128)} %get-tuple-element.52) | data formatting | bytes 36864 | tf_op jit(solution)/shard_map/slice | solution.py:17
  82.7 1.2 %copy.196 = f32[8,8,36,2]{2,1,3,0:T(8,128)} copy(f32[8,8,36,2]{3,1,2,0:T(8,128)S(1)} %get-tuple-element.53) | data formatting | bytes 36864 | tf_op jit(solution)/shard_map/slice | solution.py:18
  83.9 3.4 %collective-permute-start.3 = (f32[8,8,36,2]{2,1,3,0:T(8,128)}, f32[8,8,36,2]{2,1,3,0:T(8,128)}, u32[]{:S(2)}, u32[]{:S(2)}) collective-permute-start(f32[8,8,36,2]{2,1,3,0:T(8,128)} %copy.196), channel_id=1, source_target_pairs={{1,0},{2,1},{3,2},{4,3},{5,4},{6,5},{7,6},{0,7},{9,8},{10,9},{11,1... | collective-permute-start | bytes 55304 | tf_op jit(solution)/shard_map/ppermute | solution.py:20
  87.3 0.7 constant_dynamic-update-slice_fusion.15
  88.0 0.7 constant_dynamic-update-slice_fusion.14
  88.8 0.7 constant_dynamic-update-slice_fusion.13
  90.4 1.1 copy-done.15
  91.8 1.2 %multiply_subtract_fusion.2 = f32[8,8,33,128]{3,1,2,0:T(8,128)} fusion(f32[8,8,33,128]{3,1,2,0:T(8,128)S(1)} %get-tuple-element.93, f32[8,8,33,128]{3,1,2,0:T(8,128)S(1)} %get-tuple-element.92, f32[8,8,33,128]{3,1,2,0:T(8,128)S(1)} %get-tuple-element.60, f32[8,8,33,128]{3,1,2,0:T(8,128)S(1)} %copy-done.19, f32[8,33,128]{2,0,1:T(8,128)S(1)} %get-tuple-element.5), kind=kLoop, calls=%fused_computation.29 | loop fusion | flops 1351680 | bytes 5541888 | tf_op jit(solution)/shard_map/sub | solution.py:74
  92.9 1.5 %copy.195 = f32[8,8,36,2]{3,1,2,0:T(8,128)S(1)} copy(f32[8,8,36,2]{2,1,3,0:T(8,128)} %collective-permute-done.2) | data formatting | bytes 36864 | tf_op jit(solution)/shard_map/ppermute | solution.py:19
  94.5 1.4 %copy.198 = f32[8,8,36,2]{3,1,2,0:T(8,128)S(1)} copy(f32[8,8,36,2]{2,1,3,0:T(8,128)} %collective-permute-done.3) | data formatting | bytes 36864 | tf_op jit(solution)/shard_map/ppermute | solution.py:20
  95.9 1.0 pad_maximum_fusion
  97.5 1.4 %minimum_multiply_fusion.1 = f32[8,8,32,130]{3,1,2,0:T(8,128)S(1)} fusion(f32[8,8,32,131]{3,1,2,0:T(8,128)S(1)} %slice_subtract_fusion), kind=kLoop, calls=%fused_computation.16 | loop fusion | flops 2129920 | bytes 3194880 | tf_op jit(solution)/shard_map/mul | solution.py:63
  99.0 1.5 %fusion.3 = (f32[8,8,32,129]{3,1,2,0:T(8,128)S(1)}, f32[8,8,32,129]{3,1,2,0:T(8,128)S(1)}) fusion(f32[8,8,32,130]{3,1,2,0:T(8,128)S(1)} %minimum_multiply_fusion.1, f32[8,8,36,128]{3,1,2,0:T(8,128)S(1)} %copy-done.3, f32[8,8,36,2]{3,1,2,0:T(8,128)S(1)} %copy.195, f32[8,8,36,2]{3,1,2,0:T(8,128)S(1)} %copy.198), kind=kLoop, calls=%fused_computation.9 | loop fusion | flops 1585152 | bytes 5443584 | tf_op jit(solution)/shard_map/add | solution.py:86
  105.1 4.8 %fusion.12 = f32[8,8,32,128]{3,1,2,0:T(8,128)S(1)} fusion(f32[8,9,32,128]{3,1,2,0:T(8,128)S(1)} %copy-done.7, f32[8,8,32,129]{3,1,2,0:T(8,128)S(1)} %multiply_subtract_fusion.1, f32[8,8,33,128]{3,1,2,0:T(8,128)S(1)} %copy-done.6, f32[8,8,32,128]{3,2,1,0:T(8,128)S(1)} %copy-done.20, f32[8,8,32,128]{3,2,1,0:T(8,128)} %slice_dynamic-update-slice_fusion.6, ...), kind=kLoop, calls=%fused_computation.37 | loop fusion | flops 2883584 | bytes 10485760 | tf_op jit(solution)/shard_map/add | solution.py:116
  109.9 1.2 %copy.207 = f32[8,8,32,128]{3,2,1,0:T(8,128)} copy(f32[8,8,32,128]{3,1,2,0:T(8,128)S(1)} %fusion.12) | data formatting | bytes 2097152 | tf_op jit(solution)/shard_map/add | solution.py:116
  (116 shorter events, 14.4 us)
Async XLA Ops:
  0.0 8.2 %copy-start.1 = (f32[8,8,32,128]{3,2,1,0:T(8,128)S(1)}, f32[8,8,32,128]{3,2,1,0:T(8,128)}, u32[]{:S(2)}) copy-start(f32[8,8,32,128]{3,2,1,0:T(8,128)} %param.5) | copy-start | bytes 3145732
  1.9 1.0 copy-start.4
  3.6 39.4 %collective-permute-start.1 = (f32[8,8,2,128]{3,1,2,0:T(8,128)}, f32[8,8,2,128]{3,1,2,0:T(8,128)S(1)}, u32[]{:S(2)}, u32[]{:S(2)}) collective-permute-start(f32[8,8,2,128]{3,1,2,0:T(8,128)} %get-tuple-element.78), channel_id=1, source_target_pairs={{8,0},{16,8},{24,16},{0,24},{9,1},{17,9},{25,17},{1,25},{10,2},{18... | collective-permute-start | bytes 196616 | tf_op jit(solution)/shard_map/ppermute | solution.py:20
  7.5 50.6 %collective-permute-start = (f32[8,8,2,128]{3,1,2,0:T(8,128)}, f32[8,8,2,128]{3,1,2,0:T(8,128)S(1)}, u32[]{:S(2)}, u32[]{:S(2)}) collective-permute-start(f32[8,8,2,128]{3,1,2,0:T(8,128)} %get-tuple-element.79), channel_id=1, source_target_pairs={{0,8},{8,16},{16,24},{24,0},{1,9},{9,17},{17,25},{25,1},{2,10},{10... | collective-permute-start | bytes 196616 | tf_op jit(solution)/shard_map/ppermute | solution.py:19
  14.5 1.5 %copy-start.8 = (f32[8,9,32,128]{3,2,1,0:T(8,128)S(1)}, f32[8,9,32,128]{3,2,1,0:T(8,128)}, u32[]{:S(2)}) copy-start(f32[8,9,32,128]{3,2,1,0:T(8,128)} %get-tuple-element.80) | copy-start | bytes 3538948
  14.5 1.6 %copy-start.9 = (f32[8,9,32,128]{3,2,1,0:T(8,128)S(1)}, f32[8,9,32,128]{3,2,1,0:T(8,128)}, u32[]{:S(2)}) copy-start(f32[8,9,32,128]{3,2,1,0:T(8,128)} %get-tuple-element.81) | copy-start | bytes 3538948
  18.3 8.5 %copy-start = (f32[8,9,32,128]{3,1,2,0:T(8,128)}, f32[8,9,32,128]{3,1,2,0:T(8,128)S(1)}, u32[]{:S(2)}) copy-start(f32[8,9,32,128]{3,1,2,0:T(8,128)S(1)} %get-tuple-element.48) | copy-start | bytes 3538948
  21.3 3.2 %copy-start.10 = (f32[8,9,32,128]{3,1,2,0:T(8,128)}, f32[8,9,32,128]{3,1,2,0:T(8,128)S(1)}, u32[]{:S(2)}) copy-start(f32[8,9,32,128]{3,1,2,0:T(8,128)S(1)} %get-tuple-element.43) | copy-start | bytes 3538948
  25.4 5.2 %copy-start.12 = (f32[8,9,32,128]{3,1,2,0:T(8,128)}, f32[8,9,32,128]{3,1,2,0:T(8,128)S(1)}, u32[]{:S(2)}) copy-start(f32[8,9,32,128]{3,1,2,0:T(8,128)S(1)} %get-tuple-element.45) | copy-start | bytes 3538948
  32.9 5.4 %copy-start.11 = (f32[8,9,32,128]{3,1,2,0:T(8,128)S(1)}, f32[8,9,32,128]{3,1,2,0:T(8,128)}, u32[]{:S(2)}) copy-start(f32[8,9,32,128]{3,1,2,0:T(8,128)} %copy-done.10) | copy-start | bytes 3538948
  32.9 5.4 %copy-start.13 = (f32[8,9,32,128]{3,1,2,0:T(8,128)S(1)}, f32[8,9,32,128]{3,1,2,0:T(8,128)}, u32[]{:S(2)}) copy-start(f32[8,9,32,128]{3,1,2,0:T(8,128)} %copy-done.12) | copy-start | bytes 3538948
  73.2 1.2 %copy-start.5 = (f32[8,8,32,128]{3,1,2,0:T(8,128)S(1)}, f32[8,8,32,128]{3,1,2,0:T(8,128)}, u32[]{:S(2)}) copy-start(f32[8,8,32,128]{3,1,2,0:T(8,128)} %copy-done.4) | copy-start | bytes 3145732
  74.3 4.8 %copy-start.2 = (f32[8,8,36,128]{3,1,2,0:T(8,128)}, f32[8,8,36,128]{3,1,2,0:T(8,128)S(1)}, u32[]{:S(2)}) copy-start(f32[8,8,36,128]{3,1,2,0:T(8,128)S(1)} %get-tuple-element.87) | copy-start | bytes 3538948
  76.9 1.2 %copy-start.18 = (f32[8,8,33,128]{3,1,2,0:T(8,128)}, f32[8,8,33,128]{3,1,2,0:T(8,128)S(1)}, u32[]{:S(2)}) copy-start(f32[8,8,33,128]{3,1,2,0:T(8,128)S(1)} %get-tuple-element.8) | copy-start | bytes 3244036
  78.1 1.0 copy-start.16
  82.3 10.7 %collective-permute-start.2 = (f32[8,8,36,2]{2,1,3,0:T(8,128)S(1)}, f32[8,8,36,2]{2,1,3,0:T(8,128)}, u32[]{:S(2)}, u32[]{:S(2)}) collective-permute-start(f32[8,8,36,2]{2,1,3,0:T(8,128)S(1)} %copy.194), channel_id=1, source_target_pairs={{0,1},{1,2},{2,3},{3,4},{4,5},{5,6},{6,7},{7,0},{8,9},{9,10},{10,1... | collective-permute-start | bytes 55304 | tf_op jit(solution)/shard_map/ppermute | solution.py:19
  83.9 5.6 %copy-start.22 = (f32[1,8,33,128]{3,1,2,0:T(8,128)S(1)}, f32[1,8,33,128]{3,1,2,0:T(8,128)}, u32[]{:S(2)}) copy-start(f32[1,8,33,128]{3,1,2,0:T(8,128)} %get-tuple-element.9) | copy-start | bytes 405508
  83.9 6.3 %copy-start.14 = (f32[8,8,33,128]{3,1,2,0:T(8,128)S(1)}, f32[8,8,33,128]{3,1,2,0:T(8,128)}, u32[]{:S(2)}) copy-start(f32[8,8,33,128]{3,1,2,0:T(8,128)} %get-tuple-element.66) | copy-start | bytes 3244036
  83.9 6.3 %copy-start.17 = (f32[8,8,33,128]{3,1,2,0:T(8,128)S(1)}, f32[8,8,33,128]{3,1,2,0:T(8,128)}, u32[]{:S(2)}) copy-start(f32[8,8,33,128]{3,1,2,0:T(8,128)} %copy-done.16) | copy-start | bytes 3244036
  83.9 10.6 %collective-permute-start.3 = (f32[8,8,36,2]{2,1,3,0:T(8,128)}, f32[8,8,36,2]{2,1,3,0:T(8,128)}, u32[]{:S(2)}, u32[]{:S(2)}) collective-permute-start(f32[8,8,36,2]{2,1,3,0:T(8,128)} %copy.196), channel_id=1, source_target_pairs={{1,0},{2,1},{3,2},{4,3},{5,4},{6,5},{7,6},{0,7},{9,8},{10,9},{11,1... | collective-permute-start | bytes 55304 | tf_op jit(solution)/shard_map/ppermute | solution.py:20
  88.8 1.6 %copy-start.21 = (f32[1,8,33,128]{3,1,2,0:T(8,128)S(1)}, f32[1,8,33,128]{3,1,2,0:T(8,128)}, u32[]{:S(2)}) copy-start(f32[1,8,33,128]{3,1,2,0:T(8,128)} %get-tuple-element.11) | copy-start | bytes 405508
  90.2 1.2 %copy-start.15 = (f32[8,8,33,128]{3,1,2,0:T(8,128)S(1)}, f32[8,8,33,128]{3,1,2,0:T(8,128)}, u32[]{:S(2)}) copy-start(f32[8,8,33,128]{3,1,2,0:T(8,128)} %constant_dynamic-update-slice_fusion.21) | copy-start | bytes 3244036
  90.2 1.6 %copy-start.19 = (f32[8,8,33,128]{3,1,2,0:T(8,128)S(1)}, f32[8,8,33,128]{3,1,2,0:T(8,128)}, u32[]{:S(2)}) copy-start(f32[8,8,33,128]{3,1,2,0:T(8,128)} %get-tuple-element.54) | copy-start | bytes 3244036
  92.9 2.9 %copy-start.3 = (f32[8,8,36,128]{3,1,2,0:T(8,128)S(1)}, f32[8,8,36,128]{3,1,2,0:T(8,128)}, u32[]{:S(2)}) copy-start(f32[8,8,36,128]{3,1,2,0:T(8,128)} %copy-done.2) | copy-start | bytes 3538948
  102.9 1.2 %copy-start.6 = (f32[8,8,33,128]{3,1,2,0:T(8,128)S(1)}, f32[8,8,33,128]{3,1,2,0:T(8,128)}, u32[]{:S(2)}) copy-start(f32[8,8,33,128]{3,1,2,0:T(8,128)} %multiply_subtract_fusion.2) | copy-start | bytes 3244036
  102.9 1.9 %copy-start.7 = (f32[8,9,32,128]{3,1,2,0:T(8,128)S(1)}, f32[8,9,32,128]{3,1,2,0:T(8,128)}, u32[]{:S(2)}) copy-start(f32[8,9,32,128]{3,1,2,0:T(8,128)} %multiply_subtract_fusion) | copy-start | bytes 3538948
  102.9 2.2 %copy-start.20 = (f32[8,8,32,128]{3,2,1,0:T(8,128)S(1)}, f32[8,8,32,128]{3,2,1,0:T(8,128)}, u32[]{:S(2)}) copy-start(f32[8,8,32,128]{3,2,1,0:T(8,128)} %param.4) | copy-start | bytes 3145732
where the time goes:
time: 112 us; the launch traced here: 111 us
  other arithmetic  43.6 us (39%)
  blocking collectives  30.1 us (27%)
  local copies, waits for them, and re-layouts  27.7 us (25%)
  starting transfers between devices  7.7 us (7%)
  between operations  1.96 us (2%)
    all_gather x1, blocking collectives, on_device(): lax.all_gather(inner_src, 'gy', axis=3, tiled=True)  15.1 us
    all_gather x1, blocking collectives, on_device(): lax.all_gather(outer_src, 'gy', axis=3, tiled=True)  15 us
    unnamed x50, other arithmetic  14.1 us
    unnamed x58, local copies, waits for them, and re-layouts  14 us
    ppermute x2, starting transfers between devices, with_halo(): after = lax.ppermute(first, axis, down)  7.32 us
    sub x3, other arithmetic, rusanov(): 0.5 * (flux_left + flux_right) - 0.5 * speed * (cons_right - cons_left)  5.88 us
    add x1, other arithmetic, section_update(): return 0.5 * old + 0.5 * (conserved(core) + time_step * rates)  4.85 us
    add x3, other arithmetic, sweep(): left = take(padded, 1, length - 2) + 0.5 * take(slope, 0, length - 3)  3.84 us
  transfers between devices with their start and end apart: 4, of which 0 were waited for; matrix products, arithmetic and copies ran while one was open for 37% of the time, Pallas kernels for 0%

commit v1 on v0

--- a/solution.py
+++ b/solution.py
@@ -2,11 +2,42 @@
 import jax.numpy as jnp
 from jax import lax
 from jax.sharding import PartitionSpec as P
+from jax.lax import axis_index, axis_size, ppermute
 
 gamma_gas = 5.0 / 3.0
 omega_rate = 1.0
 shear_rate = 1.5
 time_step = 0.1
+
+
+def try_all_the_local_data(here_x, in_dim):
+    taken_in = list(here_x.shape[1:])
+    taken_in[in_dim] *= here_x.shape[0]
+    return jnp.moveaxis(here_x, 0, in_dim).reshape(taken_in)
+
+
+def serve_wall(page, which_axis, k_dim=3):
+    n = axis_size(which_axis)
+    block_list = tuple(((k0, (k0 + 1) % n) for k0 in range(n)))
+    cards = tuple(((p, src_i) for src_i, p in block_list))
+    current_value, all_rows = ([], [])
+    for j0 in range(n - 1):
+        if j0 % 2 == 0:
+            current_value.append(
+                ppermute(
+                    current_value[-1] if current_value else page,
+                    axis_name=which_axis,
+                    perm=block_list,
+                )
+            )
+        else:
+            all_rows.append(
+                ppermute(all_rows[-1] if all_rows else page, axis_name=which_axis, perm=cards)
+            )
+    out_arr = jnp.stack([*current_value[::-1], page, *all_rows], 0)
+    v_next = axis_index(which_axis) - len(current_value)
+    out_arr = out_arr[(jnp.arange(n) - v_next) % n]
+    return try_all_the_local_data(out_arr, k_dim)
 
 
 def with_halo(shard, sides, width):
@@ -127,7 +158,7 @@
     inner_src = padded[:, :, 0:2, 2:-2]
     outer_src = padded[:, :, -2:, 2:-2]
     inner_cycle, outer_cycle = (
-        lax.all_gather(inner_src, "gy", axis=3, tiled=True),
+        serve_wall(inner_src, "gy"),
         lax.all_gather(outer_src, "gy", axis=3, tiled=True),
     )
     position = lax.axis_index("gy") * cells

time: 112 us -> 116 us (1.036)
  blocking collectives: 30.1 us -> 15 us
  waiting for transfers between devices: 0.01 us -> 11.1 us
  starting transfers between devices: 7.7 us -> 15.2 us
    all_gather x1 -> x0, blocking collectives: 15.1 us -> none  [on_device(): lax.all_gather(inner_src, 'gy', axis=3, tiled=True)]
    ppermute x0 -> x7, waiting for transfers between devices: none -> 11.1 us  [the longest x4 7.54 us: serve_wall(): ppermute(current_value[-1] if current_value else page, axis_name=which_ax...]
    ppermute x0 -> x7, starting transfers between devices: none -> 7.72 us  [the longest x3 7.71 us: serve_wall(): ppermute(all_rows[-1] if all_rows else page, axis_name=which_axis, perm=c...]
    ppermute x2, starting transfers between devices: 7.32 us -> 4.54 us  [with_halo(): after = lax.ppermute(first, axis, down)]
    ppermute x2, starting transfers between devices: 0.39 us -> 2.98 us  [with_halo(): before = lax.ppermute(last, axis, up)]
    unnamed x58 -> x65, local copies, waits for them, and re-layouts: 14 us -> 14.1 us
  transfers between devices with their start and end apart: 4 -> 11, of which waited for: 0 -> 4; matrix products, arithmetic and copies ran while one was open for 37% -> 36% of each run, Pallas kernels for 0% -> 0%
where the time goes in v1:
time: 116 us; the launch traced here: 115 us
  other arithmetic  43.6 us (38%)
  local copies, waits for them, and re-layouts  28.4 us (24%)
  starting transfers between devices  15.2 us (13%)
  blocking collectives  15 us (13%)
  waiting for transfers between devices  11.1 us (10%)
  between operations  2.03 us (2%)
    all_gather x1, blocking collectives, on_device(): lax.all_gather(outer_src, 'gy', axis=3, tiled=True)  15 us
    unnamed x50, other arithmetic  14.2 us
    unnamed x65, local copies, waits for them, and re-layouts  14.1 us
    ppermute x3, starting transfers between devices, serve_wall(): ppermute(all_rows[-1] if all_rows else page, axis_name=which_axis, perm=c...  7.71 us
    ppermute x4, waiting for transfers between devices, serve_wall(): ppermute(current_value[-1] if current_value else page, axis_name=which_ax...  7.54 us
    sub x3, other arithmetic, rusanov(): 0.5 * (flux_left + flux_right) - 0.5 * speed * (cons_right - cons_left)  5.87 us
    add x1, other arithmetic, section_update(): return 0.5 * old + 0.5 * (conserved(core) + time_step * rates)  4.85 us
    ppermute x2, starting transfers between devices, with_halo(): after = lax.ppermute(first, axis, down)  4.54 us
  transfers between devices with their start and end apart: 11, of which 4 were waited for; matrix products, arithmetic and copies ran while one was open for 36% of the time, Pallas kernels for 0%

profile of v1, /device:TPU:0, one launch (start us, length us, event | category | flops | bytes accessed | tf_op | source)
XLA Modules:
  0.0 115.5 jit_solution(14060652616097353167)
XLA Ops:
  0.0 1.9 %copy.201 = f32[8,8,32,128]{3,1,2,0:T(8,128)S(1)} copy(f32[8,8,32,128]{3,2,1,0:T(8,128)} %param.5) | data formatting | bytes 2097152 | tf_op args[1]
  1.9 1.0 copy-done.4
  3.6 2.9 %collective-permute-start = (f32[8,8,2,128]{3,1,2,0:T(8,128)}, f32[8,8,2,128]{3,1,2,0:T(8,128)S(1)}, u32[]{:S(2)}, u32[]{:S(2)}) collective-permute-start(f32[8,8,2,128]{3,1,2,0:T(8,128)} %get-tuple-element.79), channel_id=1, source_target_pairs={{0,8},{8,16},{16,24},{24,0},{1,9},{9,17},{17,25},{25,1},{2,10},{10... | collective-permute-start | bytes 196616 | tf_op jit(solution)/shard_map/ppermute | solution.py:50
  6.5 1.0 collective-permute-start.8
  8.3 1.7 %pad_maximum_fusion.5 = (f32[8,9,32,128]{3,2,1,0:T(8,128)}, f32[8,9,32,128]{3,2,1,0:T(8,128)}) fusion(f32[8,8,32,128]{3,2,1,0:T(8,128)S(1)} %copy-done.1, f32[8,2,32,128]{3,2,1,0:T(8,128)S(1)} %get-tuple-element.82, f32[8,2,32,128]{3,2,1,0:T(8,128)S(1)} %get-tuple-element.83), kind=kLoop, calls=%fused_computation.20 | loop fusion | flops 589824 | bytes 3932160 | tf_op jit(solution)/shard_map/concatenate | solution.py:144
  12.4 2.1 %copy_subtract_fusion = f32[8,11,32,128]{3,1,2,0:T(8,128)S(1)} fusion(f32[8,11,32,128]{3,2,1,0:T(8,128)S(1)} %get-tuple-element.51, f32[8,11,32,128]{3,2,1,0:T(8,128)S(1)} %get-tuple-element.50), kind=kLoop, calls=%fused_computation.13 | loop fusion | flops 360448 | bytes 4325376 | tf_op jit(solution)/shard_map/sub | solution.py:115
  14.5 1.5 %minimum_multiply_fusion = f32[8,10,32,128]{3,1,2,0:T(8,128)S(1)} fusion(f32[8,11,32,128]{3,1,2,0:T(8,128)S(1)} %copy_subtract_fusion), kind=kLoop, calls=%fused_computation.15 | loop fusion | flops 2621440 | bytes 3932160 | tf_op jit(solution)/shard_map/mul | solution.py:94
  16.1 2.2 %fusion.1 = (f32[8,9,32,128]{3,1,2,0:T(8,128)S(1)}, f32[8,9,32,128]{3,1,2,0:T(8,128)S(1)}) fusion(f32[8,10,32,128]{3,1,2,0:T(8,128)S(1)} %minimum_multiply_fusion, f32[8,9,32,128]{3,2,1,0:T(8,128)S(1)} %copy-done.8, f32[8,9,32,128]{3,2,1,0:T(8,128)S(1)} %copy-done.9), kind=kLoop, calls=%fused_computation.5 | loop fusion | flops 1179648 | bytes 7077888 | tf_op jit(solution)/shard_map/add | solution.py:117
  18.5 1.4 %multiply_bitcast_fusion = (f32[9,32,128]{2,0,1:T(8,128)}, f32[1,9,32,128]{3,1,2,0:T(8,128)S(1)}, f32[1,9,32,128]{3,1,2,0:T(8,128)S(1)}, f32[8,9,32,128]{3,1,2,0:T(8,128)S(1)}) fusion(f32[8,9,32,128]{3,1,2,0:T(8,128)S(1)} %get-tuple-element.49, f32[8,9,32,128]{3,1,2,0:T(8,128)S(1)} %get-tuple-element.48, ...), kind=kLoop, calls=%fused_computation.54 | loop fusion | flops 1622016 | bytes 4341760 | tf_op jit(solution)/shard_map/mul | solution.py:105
  20.5 0.7 subtract_dynamic-update-slice_fusion
  21.2 0.8 constant_dynamic-update-slice_fusion.59
  23.6 0.9 subtract_dynamic-update-slice_fusion.9
  25.4 0.8 constant_dynamic-update-slice_fusion.64
  26.9 0.8 constant_dynamic-update-slice_fusion.62
  28.4 0.7 constant_dynamic-update-slice_fusion.71
  29.8 0.8 constant_dynamic-update-slice_fusion.69
  31.2 0.8 constant_dynamic-update-slice_fusion.67
  32.0 0.8 slice_dynamic-update-slice_fusion.6
  33.5 2.2 %constant_dynamic-update-slice_fusion.61 = f32[8,9,32,128]{3,1,2,0:T(8,128)} fusion(f32[8,9,32,128]{3,1,2,0:T(8,128)} %constant_dynamic-update-slice_fusion.62, f32[1,9,32,128]{3,1,2,0:T(8,128)} %get-tuple-element.25), kind=kLoop, calls=%fused_computation.159 | loop fusion | bytes 524288
  35.7 2.5 %slice_dynamic-update-slice_fusion = (f32[8,9,32,128]{3,1,2,0:T(8,128)}, f32[8,9,32,128]{3,1,2,0:T(8,128)}) fusion(f32[8,9,32,128]{3,1,2,0:T(8,128)} %constant_dynamic-update-slice_fusion.61, f32[8,9,32,128]{3,1,2,0:T(8,128)} %copy-done, f32[8,9,32,128]{3,1,2,0:T(8,128)} %constant_dynamic-update-slice_fusion.56, f32[8,9,32,128]{3,1,2,0:T(8,128)S(1)} %get-tuple-element.49), kind=kLoop, calls=%fused_computation.42 | loop fusion | bytes 2801664 | tf_op jit(solution)/shard_map/stack | solution.py:61
  38.2 4.1 %multiply_subtract_fusion = f32[8,9,32,128]{3,1,2,0:T(8,128)} fusion(f32[8,9,32,128]{3,1,2,0:T(8,128)} %get-tuple-element.89, f32[8,9,32,128]{3,1,2,0:T(8,128)} %get-tuple-element.88, f32[8,9,32,128]{3,1,2,0:T(8,128)S(1)} %copy-done.13, f32[8,9,32,128]{3,1,2,0:T(8,128)S(1)} %copy-done.11, f32[9,32,128]{2,0,1:T(8,128)} %get-tuple-element.19), kind=kLoop, calls=%fused_computation.14 | loop fusion | flops 1474560 | bytes 6045696 | tf_op jit(solution)/shard_map/sub | solution.py:105
  43.0 5.5 %collective-permute-done.1 = f32[8,8,2,128]{3,1,2,0:T(8,128)S(1)} collective-permute-done((f32[8,8,2,128]{3,1,2,0:T(8,128)S(1)}, f32[8,8,2,128]{3,1,2,0:T(8,128)S(1)}, u32[]{:S(2)}, u32[]{:S(2)}) %collective-permute-start.1) | collective-permute-done | bytes 65568 | tf_op jit(solution)/shard_map/ppermute | solution.py:27
  48.4 3.5 %collective-permute-start.5 = (f32[8,8,2,128]{3,1,2,0:T(8,128)S(1)}, f32[8,8,2,128]{3,1,2,0:T(8,128)S(1)}, u32[]{:S(2)}, u32[]{:S(2)}) collective-permute-start(f32[8,8,2,128]{3,1,2,0:T(8,128)S(1)} %collective-permute-done), channel_id=1, source_target_pairs={{1,0},{2,1},{3,2},{4,3},{5,4},{6,5},{7,6},{0,7},{9,8},{10,9},{11,1... | collective-permute-start | bytes 196616 | tf_op jit(solution)/shard_map/ppermute | solution.py:35
  52.0 2.0 %collective-permute-done.2 = f32[8,8,2,128]{3,1,2,0:T(8,128)S(1)} collective-permute-done((f32[8,8,2,128]{3,1,2,0:T(8,128)S(1)}, f32[8,8,2,128]{3,1,2,0:T(8,128)S(1)}, u32[]{:S(2)}, u32[]{:S(2)}) %collective-permute-start.2) | collective-permute-done | bytes 65568 | tf_op jit(solution)/shard_map/ppermute | solution.py:27
  54.0 15.0 %all_gather.3 = f32[8,8,2,1024]{3,1,2,0:T(8,128)S(1)} all-gather(f32[8,8,2,128]{3,1,2,0:T(8,128)S(1)} %collective-permute-done.8), channel_id=1, replica_groups=mesh['gx'=4,'gy'=8] {'gy'}, dimensions={3}, use_global_device_ids=true | all-gather | bytes 589824 | tf_op jit(solution)/shard_map/all_gather | solution.py:162
  69.8 1.7 %collective-permute-done.6 = f32[8,8,2,128]{3,1,2,0:T(8,128)S(1)} collective-permute-done((f32[8,8,2,128]{3,1,2,0:T(8,128)S(1)}, f32[8,8,2,128]{3,1,2,0:T(8,128)S(1)}, u32[]{:S(2)}, u32[]{:S(2)}) %collective-permute-start.6) | collective-permute-done | bytes 65568 | tf_op jit(solution)/shard_map/ppermute | solution.py:35
  71.6 3.6 %collective-permute-start.7 = (f32[8,8,2,128]{3,1,2,0:T(8,128)S(1)}, f32[8,8,2,128]{3,1,2,0:T(8,128)S(1)}, u32[]{:S(2)}, u32[]{:S(2)}) collective-permute-start(f32[8,8,2,128]{3,1,2,0:T(8,128)S(1)} %collective-permute-done.6), channel_id=1, source_target_pairs={{1,0},{2,1},{3,2},{4,3},{5,4},{6,5},{7,6},{0,7},{9,8},{10,9},{11,1... | collective-permute-start | bytes 196616 | tf_op jit(solution)/shard_map/ppermute | solution.py:35
  75.3 1.8 %collective-permute-done.7 = f32[8,8,2,128]{3,1,2,0:T(8,128)S(1)} collective-permute-done((f32[8,8,2,128]{3,1,2,0:T(8,128)S(1)}, f32[8,8,2,128]{3,1,2,0:T(8,128)S(1)}, u32[]{:S(2)}, u32[]{:S(2)}) %collective-permute-start.7) | collective-permute-done | bytes 65568 | tf_op jit(solution)/shard_map/ppermute | solution.py:35
  79.7 0.9 multiply_bitcast_fusion.2
  80.7 0.7 constant_dynamic-update-slice_fusion.24
  81.6 1.0 constant_dynamic-update-slice_fusion.16
  82.6 1.0 copy-done.16
  83.6 1.4 %fusion.23 = (f32[8,8,36,2]{3,1,2,0:T(8,128)}, f32[8,8,36,2]{3,1,2,0:T(8,128)S(1)}) fusion(f32[8,8,36,128]{3,1,2,0:T(8,128)S(1)} %get-tuple-element.87), kind=kLoop, calls=%fused_computation.222 | loop fusion | bytes 73728 | tf_op jit(solution)/shard_map/slice | solution.py:48
  85.0 1.8 %copy.208 = f32[8,8,36,2]{2,1,3,0:T(8,128)S(1)} copy(f32[8,8,36,2]{3,1,2,0:T(8,128)} %get-tuple-element.52) | data formatting | bytes 36864 | tf_op jit(solution)/shard_map/slice | solution.py:48
  86.9 1.2 %copy.210 = f32[8,8,36,2]{2,1,3,0:T(8,128)} copy(f32[8,8,36,2]{3,1,2,0:T(8,128)S(1)} %get-tuple-element.53) | data formatting | bytes 36864 | tf_op jit(solution)/shard_map/slice | solution.py:49
  88.0 3.6 %collective-permute-start.10 = (f32[8,8,36,2]{2,1,3,0:T(8,128)}, f32[8,8,36,2]{2,1,3,0:T(8,128)}, u32[]{:S(2)}, u32[]{:S(2)}) collective-permute-start(f32[8,8,36,2]{2,1,3,0:T(8,128)} %copy.210), channel_id=1, source_target_pairs={{1,0},{2,1},{3,2},{4,3},{5,4},{6,5},{7,6},{0,7},{9,8},{10,9},{11,1... | collective-permute-start | bytes 55304 | tf_op jit(solution)/shard_map/ppermute | solution.py:51
  91.6 0.7 constant_dynamic-update-slice_fusion.23
  92.4 0.8 constant_dynamic-update-slice_fusion.22
  93.1 0.8 constant_dynamic-update-slice_fusion.21
  94.7 1.1 copy-done.15
  96.1 1.2 %multiply_subtract_fusion.2 = f32[8,8,33,128]{3,1,2,0:T(8,128)} fusion(f32[8,8,33,128]{3,1,2,0:T(8,128)S(1)} %get-tuple-element.93, f32[8,8,33,128]{3,1,2,0:T(8,128)S(1)} %get-tuple-element.92, f32[8,8,33,128]{3,1,2,0:T(8,128)S(1)} %get-tuple-element.60, f32[8,8,33,128]{3,1,2,0:T(8,128)S(1)} %copy-done.19, f32[8,33,128]{2,0,1:T(8,128)S(1)} %get-tuple-element.5), kind=kLoop, calls=%fused_computation.30 | loop fusion | flops 1351680 | bytes 5541888 | tf_op jit(solution)/shard_map/sub | solution.py:105
  97.3 1.5 %copy.209 = f32[8,8,36,2]{3,1,2,0:T(8,128)S(1)} copy(f32[8,8,36,2]{2,1,3,0:T(8,128)} %collective-permute-done.9) | data formatting | bytes 36864 | tf_op jit(solution)/shard_map/ppermute | solution.py:50
  98.9 1.4 %copy.212 = f32[8,8,36,2]{3,1,2,0:T(8,128)S(1)} copy(f32[8,8,36,2]{2,1,3,0:T(8,128)} %collective-permute-done.10) | data formatting | bytes 36864 | tf_op jit(solution)/shard_map/ppermute | solution.py:51
  100.3 1.0 pad_maximum_fusion
  101.9 1.4 %minimum_multiply_fusion.1 = f32[8,8,32,130]{3,1,2,0:T(8,128)S(1)} fusion(f32[8,8,32,131]{3,1,2,0:T(8,128)S(1)} %slice_subtract_fusion), kind=kLoop, calls=%fused_computation.17 | loop fusion | flops 2129920 | bytes 3194880 | tf_op jit(solution)/shard_map/mul | solution.py:94
  103.3 1.5 %fusion.3 = (f32[8,8,32,129]{3,1,2,0:T(8,128)S(1)}, f32[8,8,32,129]{3,1,2,0:T(8,128)S(1)}) fusion(f32[8,8,32,130]{3,1,2,0:T(8,128)S(1)} %minimum_multiply_fusion.1, f32[8,8,36,128]{3,1,2,0:T(8,128)S(1)} %copy-done.3, f32[8,8,36,2]{3,1,2,0:T(8,128)S(1)} %copy.209, f32[8,8,36,2]{3,1,2,0:T(8,128)S(1)} %copy.212), kind=kLoop, calls=%fused_computation.10 | loop fusion | flops 1585152 | bytes 5443584 | tf_op jit(solution)/shard_map/add | solution.py:117
  109.4 4.8 %fusion.12 = f32[8,8,32,128]{3,1,2,0:T(8,128)S(1)} fusion(f32[8,9,32,128]{3,1,2,0:T(8,128)S(1)} %copy-done.7, f32[8,8,32,129]{3,1,2,0:T(8,128)S(1)} %multiply_subtract_fusion.1, f32[8,8,33,128]{3,1,2,0:T(8,128)S(1)} %copy-done.6, f32[8,8,32,128]{3,2,1,0:T(8,128)S(1)} %copy-done.20, f32[8,8,32,128]{3,2,1,0:T(8,128)} %slice_dynamic-update-slice_fusion.6, ...), kind=kLoop, calls=%fused_computation.38 | loop fusion | flops 2883584 | bytes 10485760 | tf_op jit(solution)/shard_map/add | solution.py:147
  114.3 1.2 %copy.221 = f32[8,8,32,128]{3,2,1,0:T(8,128)} copy(f32[8,8,32,128]{3,1,2,0:T(8,128)S(1)} %fusion.12) | data formatting | bytes 2097152 | tf_op jit(solution)/shard_map/add | solution.py:147
  (141 shorter events, 19.9 us)
Async XLA Ops:
  0.0 8.2 %copy-start.1 = (f32[8,8,32,128]{3,2,1,0:T(8,128)S(1)}, f32[8,8,32,128]{3,2,1,0:T(8,128)}, u32[]{:S(2)}) copy-start(f32[8,8,32,128]{3,2,1,0:T(8,128)} %param.5) | copy-start | bytes 3145732
  1.9 1.0 copy-start.4
  3.6 39.4 %collective-permute-start = (f32[8,8,2,128]{3,1,2,0:T(8,128)}, f32[8,8,2,128]{3,1,2,0:T(8,128)S(1)}, u32[]{:S(2)}, u32[]{:S(2)}) collective-permute-start(f32[8,8,2,128]{3,1,2,0:T(8,128)} %get-tuple-element.79), channel_id=1, source_target_pairs={{0,8},{8,16},{16,24},{24,0},{1,9},{9,17},{17,25},{25,1},{2,10},{10... | collective-permute-start | bytes 196616 | tf_op jit(solution)/shard_map/ppermute | solution.py:50
  6.5 47.6 %collective-permute-start.8 = (f32[8,8,2,128]{3,1,2,0:T(8,128)}, f32[8,8,2,128]{3,1,2,0:T(8,128)S(1)}, u32[]{:S(2)}, u32[]{:S(2)}) collective-permute-start(f32[8,8,2,128]{3,1,2,0:T(8,128)} %get-tuple-element.78), channel_id=1, source_target_pairs={{8,0},{16,8},{24,16},{0,24},{9,1},{17,9},{25,17},{1,25},{10,2},{18... | collective-permute-start | bytes 196616 | tf_op jit(solution)/shard_map/ppermute | solution.py:51
  14.5 1.5 %copy-start.8 = (f32[8,9,32,128]{3,2,1,0:T(8,128)S(1)}, f32[8,9,32,128]{3,2,1,0:T(8,128)}, u32[]{:S(2)}) copy-start(f32[8,9,32,128]{3,2,1,0:T(8,128)} %get-tuple-element.80) | copy-start | bytes 3538948
  14.5 1.6 %copy-start.9 = (f32[8,9,32,128]{3,2,1,0:T(8,128)S(1)}, f32[8,9,32,128]{3,2,1,0:T(8,128)}, u32[]{:S(2)}) copy-start(f32[8,9,32,128]{3,2,1,0:T(8,128)} %get-tuple-element.81) | copy-start | bytes 3538948
  18.3 8.6 %copy-start = (f32[8,9,32,128]{3,1,2,0:T(8,128)}, f32[8,9,32,128]{3,1,2,0:T(8,128)S(1)}, u32[]{:S(2)}) copy-start(f32[8,9,32,128]{3,1,2,0:T(8,128)S(1)} %get-tuple-element.48) | copy-start | bytes 3538948
  21.2 3.3 %copy-start.10 = (f32[8,9,32,128]{3,1,2,0:T(8,128)}, f32[8,9,32,128]{3,1,2,0:T(8,128)S(1)}, u32[]{:S(2)}) copy-start(f32[8,9,32,128]{3,1,2,0:T(8,128)S(1)} %get-tuple-element.43) | copy-start | bytes 3538948
  25.4 5.2 %copy-start.12 = (f32[8,9,32,128]{3,1,2,0:T(8,128)}, f32[8,9,32,128]{3,1,2,0:T(8,128)S(1)}, u32[]{:S(2)}) copy-start(f32[8,9,32,128]{3,1,2,0:T(8,128)S(1)} %get-tuple-element.45) | copy-start | bytes 3538948
  32.8 5.4 %copy-start.11 = (f32[8,9,32,128]{3,1,2,0:T(8,128)S(1)}, f32[8,9,32,128]{3,1,2,0:T(8,128)}, u32[]{:S(2)}) copy-start(f32[8,9,32,128]{3,1,2,0:T(8,128)} %copy-done.10) | copy-start | bytes 3538948
  32.8 5.4 %copy-start.13 = (f32[8,9,32,128]{3,1,2,0:T(8,128)S(1)}, f32[8,9,32,128]{3,1,2,0:T(8,128)}, u32[]{:S(2)}) copy-start(f32[8,9,32,128]{3,1,2,0:T(8,128)} %copy-done.12) | copy-start | bytes 3538948
  42.9 5.5 %collective-permute-start.1 = (f32[8,8,2,128]{3,1,2,0:T(8,128)S(1)}, f32[8,8,2,128]{3,1,2,0:T(8,128)S(1)}, u32[]{:S(2)}, u32[]{:S(2)}) collective-permute-start(f32[8,8,2,128]{3,1,2,0:T(8,128)S(1)} %collective-permute-done), channel_id=1, source_target_pairs={{0,1},{1,2},{2,3},{3,4},{4,5},{5,6},{6,7},{7,0},{8,9},{9,10},{10,1... | collective-permute-start | bytes 196616 | tf_op jit(solution)/shard_map/ppermute | solution.py:27
  48.4 5.6 %collective-permute-start.2 = (f32[8,8,2,128]{3,1,2,0:T(8,128)S(1)}, f32[8,8,2,128]{3,1,2,0:T(8,128)S(1)}, u32[]{:S(2)}, u32[]{:S(2)}) collective-permute-start(f32[8,8,2,128]{3,1,2,0:T(8,128)S(1)} %collective-permute-done.1), channel_id=1, source_target_pairs={{0,1},{1,2},{2,3},{3,4},{4,5},{5,6},{6,7},{7,0},{8,9},{9,10},{10,1... | collective-permute-start | bytes 196616 | tf_op jit(solution)/shard_map/ppermute | solution.py:27
  48.4 20.6 %collective-permute-start.5 = (f32[8,8,2,128]{3,1,2,0:T(8,128)S(1)}, f32[8,8,2,128]{3,1,2,0:T(8,128)S(1)}, u32[]{:S(2)}, u32[]{:S(2)}) collective-permute-start(f32[8,8,2,128]{3,1,2,0:T(8,128)S(1)} %collective-permute-done), channel_id=1, source_target_pairs={{1,0},{2,1},{3,2},{4,3},{5,4},{6,5},{7,6},{0,7},{9,8},{10,9},{11,1... | collective-permute-start | bytes 196616 | tf_op jit(solution)/shard_map/ppermute | solution.py:35
  54.0 15.6 %collective-permute-start.3 = (f32[8,8,2,128]{3,1,2,0:T(8,128)S(1)}, f32[8,8,2,128]{3,1,2,0:T(8,128)S(1)}, u32[]{:S(2)}, u32[]{:S(2)}) collective-permute-start(f32[8,8,2,128]{3,1,2,0:T(8,128)S(1)} %collective-permute-done.2), channel_id=1, source_target_pairs={{0,1},{1,2},{2,3},{3,4},{4,5},{5,6},{6,7},{7,0},{8,9},{9,10},{10,1... | collective-permute-start | bytes 196616 | tf_op jit(solution)/shard_map/ppermute | solution.py:27
  69.1 2.5 %collective-permute-start.6 = (f32[8,8,2,128]{3,1,2,0:T(8,128)S(1)}, f32[8,8,2,128]{3,1,2,0:T(8,128)S(1)}, u32[]{:S(2)}, u32[]{:S(2)}) collective-permute-start(f32[8,8,2,128]{3,1,2,0:T(8,128)S(1)} %collective-permute-done.5), channel_id=1, source_target_pairs={{1,0},{2,1},{3,2},{4,3},{5,4},{6,5},{7,6},{0,7},{9,8},{10,9},{11,1... | collective-permute-start | bytes 196616 | tf_op jit(solution)/shard_map/ppermute | solution.py:35
  69.7 5.5 %collective-permute-start.4 = (f32[8,8,2,128]{3,1,2,0:T(8,128)S(1)}, f32[8,8,2,128]{3,1,2,0:T(8,128)S(1)}, u32[]{:S(2)}, u32[]{:S(2)}) collective-permute-start(f32[8,8,2,128]{3,1,2,0:T(8,128)S(1)} %collective-permute-done.3), channel_id=1, source_target_pairs={{0,1},{1,2},{2,3},{3,4},{4,5},{5,6},{6,7},{7,0},{8,9},{9,10},{10,1... | collective-permute-start | bytes 196616 | tf_op jit(solution)/shard_map/ppermute | solution.py:27
  71.6 5.5 %collective-permute-start.7 = (f32[8,8,2,128]{3,1,2,0:T(8,128)S(1)}, f32[8,8,2,128]{3,1,2,0:T(8,128)S(1)}, u32[]{:S(2)}, u32[]{:S(2)}) collective-permute-start(f32[8,8,2,128]{3,1,2,0:T(8,128)S(1)} %collective-permute-done.6), channel_id=1, source_target_pairs={{1,0},{2,1},{3,2},{4,3},{5,4},{6,5},{7,6},{0,7},{9,8},{10,9},{11,1... | collective-permute-start | bytes 196616 | tf_op jit(solution)/shard_map/ppermute | solution.py:35
  77.7 1.2 %copy-start.5 = (f32[8,8,32,128]{3,1,2,0:T(8,128)S(1)}, f32[8,8,32,128]{3,1,2,0:T(8,128)}, u32[]{:S(2)}) copy-start(f32[8,8,32,128]{3,1,2,0:T(8,128)} %copy-done.4) | copy-start | bytes 3145732
  78.7 4.9 %copy-start.2 = (f32[8,8,36,128]{3,1,2,0:T(8,128)}, f32[8,8,36,128]{3,1,2,0:T(8,128)S(1)}, u32[]{:S(2)}) copy-start(f32[8,8,36,128]{3,1,2,0:T(8,128)S(1)} %get-tuple-element.87) | copy-start | bytes 3538948
  81.5 1.1 copy-start.18
  82.6 1.0 copy-start.16
  86.8 10.5 %collective-permute-start.9 = (f32[8,8,36,2]{2,1,3,0:T(8,128)S(1)}, f32[8,8,36,2]{2,1,3,0:T(8,128)}, u32[]{:S(2)}, u32[]{:S(2)}) collective-permute-start(f32[8,8,36,2]{2,1,3,0:T(8,128)S(1)} %copy.208), channel_id=1, source_target_pairs={{0,1},{1,2},{2,3},{3,4},{4,5},{5,6},{6,7},{7,0},{8,9},{9,10},{10,1... | collective-permute-start | bytes 55304 | tf_op jit(solution)/shard_map/ppermute | solution.py:50
  88.0 5.9 %copy-start.22 = (f32[1,8,33,128]{3,1,2,0:T(8,128)S(1)}, f32[1,8,33,128]{3,1,2,0:T(8,128)}, u32[]{:S(2)}) copy-start(f32[1,8,33,128]{3,1,2,0:T(8,128)} %get-tuple-element.9) | copy-start | bytes 405508
  88.0 6.5 %copy-start.14 = (f32[8,8,33,128]{3,1,2,0:T(8,128)S(1)}, f32[8,8,33,128]{3,1,2,0:T(8,128)}, u32[]{:S(2)}) copy-start(f32[8,8,33,128]{3,1,2,0:T(8,128)} %get-tuple-element.66) | copy-start | bytes 3244036
  88.0 6.5 %copy-start.17 = (f32[8,8,33,128]{3,1,2,0:T(8,128)S(1)}, f32[8,8,33,128]{3,1,2,0:T(8,128)}, u32[]{:S(2)}) copy-start(f32[8,8,33,128]{3,1,2,0:T(8,128)} %copy-done.16) | copy-start | bytes 3244036
  88.0 10.8 %collective-permute-start.10 = (f32[8,8,36,2]{2,1,3,0:T(8,128)}, f32[8,8,36,2]{2,1,3,0:T(8,128)}, u32[]{:S(2)}, u32[]{:S(2)}) collective-permute-start(f32[8,8,36,2]{2,1,3,0:T(8,128)} %copy.210), channel_id=1, source_target_pairs={{1,0},{2,1},{3,2},{4,3},{5,4},{6,5},{7,6},{0,7},{9,8},{10,9},{11,1... | collective-permute-start | bytes 55304 | tf_op jit(solution)/shard_map/ppermute | solution.py:51
  93.1 1.6 %copy-start.21 = (f32[1,8,33,128]{3,1,2,0:T(8,128)S(1)}, f32[1,8,33,128]{3,1,2,0:T(8,128)}, u32[]{:S(2)}) copy-start(f32[1,8,33,128]{3,1,2,0:T(8,128)} %get-tuple-element.11) | copy-start | bytes 405508
  94.6 1.2 %copy-start.15 = (f32[8,8,33,128]{3,1,2,0:T(8,128)S(1)}, f32[8,8,33,128]{3,1,2,0:T(8,128)}, u32[]{:S(2)}) copy-start(f32[8,8,33,128]{3,1,2,0:T(8,128)} %constant_dynamic-update-slice_fusion.29) | copy-start | bytes 3244036
  94.6 1.6 %copy-start.19 = (f32[8,8,33,128]{3,1,2,0:T(8,128)S(1)}, f32[8,8,33,128]{3,1,2,0:T(8,128)}, u32[]{:S(2)}) copy-start(f32[8,8,33,128]{3,1,2,0:T(8,128)} %get-tuple-element.54) | copy-start | bytes 3244036
  97.3 2.9 %copy-start.3 = (f32[8,8,36,128]{3,1,2,0:T(8,128)S(1)}, f32[8,8,36,128]{3,1,2,0:T(8,128)}, u32[]{:S(2)}) copy-start(f32[8,8,36,128]{3,1,2,0:T(8,128)} %copy-done.2) | copy-start | bytes 3538948
  107.3 1.2 %copy-start.6 = (f32[8,8,33,128]{3,1,2,0:T(8,128)S(1)}, f32[8,8,33,128]{3,1,2,0:T(8,128)}, u32[]{:S(2)}) copy-start(f32[8,8,33,128]{3,1,2,0:T(8,128)} %multiply_subtract_fusion.2) | copy-start | bytes 3244036
  107.3 1.9 %copy-start.7 = (f32[8,9,32,128]{3,1,2,0:T(8,128)S(1)}, f32[8,9,32,128]{3,1,2,0:T(8,128)}, u32[]{:S(2)}) copy-start(f32[8,9,32,128]{3,1,2,0:T(8,128)} %multiply_subtract_fusion) | copy-start | bytes 3538948
  107.3 2.2 %copy-start.20 = (f32[8,8,32,128]{3,2,1,0:T(8,128)S(1)}, f32[8,8,32,128]{3,2,1,0:T(8,128)}, u32[]{:S(2)}) copy-start(f32[8,8,32,128]{3,2,1,0:T(8,128)} %param.4) | copy-start | bytes 3145732
